TPU v7x, 128 devices: a whole 4x4x4 slice. The times are simulated.
128 devices in a mesh: dp: 32 (over y, z, core), expert: 4 (over x).
Axes of the slice: x: 4, y: 4, z: 4, core: 2. Of those that a mesh axis runs over, the one named last changes fastest.
Arguments:
- local_grads: bfloat16 [4, 32, 1024, 3584], P('expert', 'dp')
- momentum: float32 [4, 1024, 3584], P('expert', None, 'dp'), may hold values from -6 to 6
Outputs:
- new_momentum: float32 [4, 1024, 3584], P('expert', None, 'dp')
- update: float32 [4, 1024, 3584], P('expert', None, 'dp')
All inputs are finite; a program needn't handle non-finite values.
Results may differ from a plain program's by a relative error of at most 0.0003.
Values sent between devices are 32-bit elements; how exact they have to be, the bound alone decides.
A program may use at most 128 MiB of HBM per device.

v0:
```python
import math

import jax
import jax.numpy as jnp
from jax import lax
from jax.sharding import Mesh
from jax.sharding import PartitionSpec as P

HID = 1024
WID = 3584
ITERS = 3
DP = ("dp_0", "dp_1", "dp_2")
DP_EXPERT = ("dp_0", "dp_1", "dp_2", "expert")


first_coef = 3.4445
second_coef = -4.775
third_coef = 2.0315
momentum_decay = 0.95


def over_axes(x, axes):
    for axis in axes:
        x = lax.psum(x, axis)
    return x


def precise(left, right):
    return jnp.dot(left, right, precision=lax.Precision.HIGHEST, preferred_element_type=jnp.float32)


def body(local_grads, momentum):
    grads = lax.psum_scatter(
        local_grads[0, 0].astype(jnp.float32), DP, scatter_dimension=1, tiled=True
    )
    count = HID * WID * lax.axis_size("expert")
    total_sq = over_axes(jnp.sum(grads * grads), DP_EXPERT)
    root_mean = jnp.sqrt(total_sq / count + 1e-06)
    factor = jnp.minimum(1.0, 1.0 / root_mean)
    clipped = factor * grads
    new_momentum = momentum_decay * momentum[0] + clipped
    iterate = clipped + momentum_decay * new_momentum
    for number in range(ITERS):
        partial_value = precise(iterate, iterate.T)
        gram = lax.psum(partial_value, DP)
        if number == 0:
            norm_scale = jnp.sqrt(jnp.trace(gram)) + 1e-07
            iterate = iterate / norm_scale
            gram = gram / (norm_scale * norm_scale)
        product = precise(gram, iterate)
        iterate = first_coef * iterate + second_coef * product + third_coef * precise(gram, product)
    update = iterate * (0.2 * math.sqrt(max(HID, WID)))
    return (new_momentum[None], update[None])


def solution(mesh):
    finer = Mesh(
        mesh.devices.reshape(4, 4, 2, mesh.shape["expert"]), ("dp_0", "dp_1", "dp_2", "expert")
    )
    in_specs = (P("expert", DP, None, None), P("expert", None, DP))
    out_specs = (P("expert", None, DP), P("expert", None, DP))
    return jax.shard_map(body, mesh=finer, in_specs=in_specs, out_specs=out_specs, check_vma=False)
```

profile of v0, /device:TPU:1, one launch (start us, length us, event | category | flops | bytes accessed | tf_op | source)
XLA Modules:
  0.0 568.9 jit_solution(17145518755255574495)
XLA Ops:
  7.2 0.0 reduce-scatter.2.cloned.1.call-start
  7.2 10.4 %copy.4 = bf16[1,1,1024,3584]{2,3,1,0:T(8,128)(2,1)} copy(bf16[1,1,1024,3584]{3,2,1,0:T(8,128)(2,1)} %param.2) | data formatting | bytes 14680064 | tf_op args[0]
  17.6 10.2 %bitcast_convert_fusion = f32[1024,3584]{0,1:T(8,128)} fusion(bf16[1,1,1024,3584]{2,3,1,0:T(8,128)(2,1)} %copy.4), kind=kLoop, calls=%fused_computation | loop fusion | flops 3670016 | bytes 22020096 | tf_op jit(solution)/shard_map/convert_element_type | solution.py:34
  27.8 0.0 copy-start.3
  27.8 0.0 reduce-scatter.2.cloned.1.call-update
  27.8 0.0 all-reduce.4.cloned.1.call-start
  27.9 112.1 %reduce-scatter.2.cloned.1.call-done = f32[1024,112]{0,1:T(8,128)} async-done(((f32[1024,3584]{0,1:T(8,128)}), f32[1024,112]{0,1:T(8,128)}) %reduce-scatter.2.cloned.1.call-update) | async-done | bytes 458768 | tf_op jit(solution)/shard_map/reduce_scatter | solution.py:33
  139.9 1.7 multiply_reduce_fusion
  141.7 8.7 %psum.49 = f32[]{:T(128)} all-reduce(f32[]{:T(128)} %multiply_reduce_fusion), channel_id=1, replica_groups=mesh['dp_0'=4,'dp_1'=4,'dp_2'=2,'expert'=4] {'dp_0'}, use_global_device_ids=true, to_apply=%region_2.0 | all-reduce | flops 1 | bytes 8 | tf_op jit(solution)/shard_map/psum | solution.py:24
  150.4 7.1 %psum.50 = f32[]{:T(128)} all-reduce(f32[]{:T(128)} %psum.49), channel_id=1, replica_groups=mesh['dp_0'=4,'dp_1'=4,'dp_2'=2,'expert'=4] {'dp_1'}, use_global_device_ids=true, to_apply=%region_3.0 | all-reduce | flops 1 | bytes 8 | tf_op jit(solution)/shard_map/psum | solution.py:24
  157.5 8.6 %psum.51 = f32[]{:T(128)} all-reduce(f32[]{:T(128)} %psum.50), channel_id=1, replica_groups=mesh['dp_0'=4,'dp_1'=4,'dp_2'=2,'expert'=4] {'dp_2'}, use_global_device_ids=true, to_apply=%region_4.0 | all-reduce | flops 1 | bytes 8 | tf_op jit(solution)/shard_map/psum | solution.py:24
  166.1 9.0 %psum.52 = f32[]{:T(128)} all-reduce(f32[]{:T(128)} %psum.51), channel_id=1, replica_groups=mesh['dp_0'=4,'dp_1'=4,'dp_2'=2,'expert'=4] {'expert'}, use_global_device_ids=true, to_apply=%region_5.0 | all-reduce | flops 1 | bytes 8 | tf_op jit(solution)/shard_map/psum | solution.py:24
  175.8 0.0 copy-done.3
  175.8 1.9 multiply_add_fusion
  177.7 5.1 fusion.9
  182.8 0.0 all-reduce.4.cloned.1.call-update
  182.8 0.2 all-reduce.6.cloned.1.call-start
  183.1 108.6 %all-reduce.4.cloned.1.call-done = f32[1024,1024]{1,0:T(8,128)} async-done(((f32[1024,1024]{1,0:T(8,128)}), f32[1024,1024]{1,0:T(8,128)}) %all-reduce.4.cloned.1.call-update) | async-done | bytes 4194320 | tf_op jit(solution)/shard_map/psum | solution.py:45
  291.6 2.9 select_reduce_fusion
  295.2 0.0 copy-start.2
  295.3 6.8 %fusion.1 = f32[1024,112]{0,1:T(8,128)S(1)} fusion(f32[1024,1024]{1,0:T(8,128)} %all-reduce.4.cloned.1.call-done, f32[]{:T(128)S(6)} %mul.61, f32[1024,112]{0,1:T(8,128)S(1)} %get-tuple-element.2, f32[]{:T(128)S(6)} %add.49), kind=kOutput, calls=%fused_computation.5 | convolution fusion | flops 1410449408 | bytes 5111816 | tf_op jit(solution)/shard_map/dot_general | solution.py:29
  302.0 0.0 copy-done.2
  302.1 4.3 fusion.7
  306.4 5.1 fusion.10
  311.5 0.0 all-reduce.6.cloned.1.call-update
  311.5 0.3 all-reduce.8.cloned.1.call-start
  311.8 111.2 %all-reduce.6.cloned.1.call-done = f32[1024,1024]{1,0:T(8,128)} async-done(((f32[1024,1024]{1,0:T(8,128)}), f32[1024,1024]{1,0:T(8,128)}) %all-reduce.6.cloned.1.call-update) | async-done | bytes 4194320 | tf_op jit(solution)/shard_map/psum | solution.py:45
  423.0 0.0 copy-start
  423.0 6.6 %fusion.11 = f32[1024,112]{0,1:T(8,128)S(1)} fusion(f32[1024,1024]{1,0:T(8,128)} %all-reduce.6.cloned.1.call-done, f32[1024,112]{0,1:T(8,128)S(1)} %fusion.7), kind=kOutput, calls=%fused_computation.21 | convolution fusion | flops 1409286144 | bytes 5111808 | tf_op jit(solution)/shard_map/dot_general | solution.py:29
  429.6 0.0 copy-done
  429.6 4.3 fusion.2
  433.9 5.3 fusion.12
  439.2 0.0 all-reduce.8.cloned.1.call-update
  439.3 111.4 %all-reduce.8.cloned.1.call-done = f32[1024,1024]{1,0:T(8,128)} async-done(((f32[1024,1024]{1,0:T(8,128)}), f32[1024,1024]{1,0:T(8,128)}) %all-reduce.8.cloned.1.call-update) | async-done | bytes 4194320 | tf_op jit(solution)/shard_map/psum | solution.py:45
  550.7 0.0 copy-start.1
  550.7 6.6 %fusion.13 = f32[1024,112]{0,1:T(8,128)S(1)} fusion(f32[1024,1024]{1,0:T(8,128)} %all-reduce.8.cloned.1.call-done, f32[1024,112]{0,1:T(8,128)S(1)} %fusion.2), kind=kOutput, calls=%fused_computation.23 | convolution fusion | flops 1409286144 | bytes 5111808 | tf_op jit(solution)/shard_map/dot_general | solution.py:29
  557.3 0.0 copy-done.1
  557.3 5.1 fusion.5
Async XLA Ops:
  7.2 132.8 %reduce-scatter.2.cloned.1.call-start = ((), (), s32[]{:S(2)}) async-start(), calls=%async_computation.1 | async-start | bytes 15138816 | tf_op jit(solution)/shard_map/reduce_scatter | solution.py:33
  27.8 148.0 %copy-start.3 = (f32[1,1024,112]{1,2,0:T(8,128)S(1)}, f32[1,1024,112]{1,2,0:T(8,128)}, u32[]{:S(2)}) copy-start(f32[1,1024,112]{1,2,0:T(8,128)} %param.3) | copy-start | bytes 1376260
  27.8 263.8 %all-reduce.4.cloned.1.call-start = ((), (), s32[]{:S(2)}) async-start(), calls=%async_computation.2 | async-start | bytes 8388608 | tf_op jit(solution)/shard_map/psum | solution.py:45
  182.8 240.2 %all-reduce.6.cloned.1.call-start = ((), (), s32[]{:S(2)}) async-start(), calls=%async_computation.3 | async-start | bytes 8388608 | tf_op jit(solution)/shard_map/psum | solution.py:45
  295.2 6.8 %copy-start.2 = (f32[1024,1024]{1,0:T(8,128)S(1)}, f32[1024,1024]{1,0:T(8,128)}, u32[]{:S(2)}) copy-start(f32[1024,1024]{1,0:T(8,128)} %all-reduce.4.cloned.1.call-done) | copy-start | bytes 12582916
  311.5 239.2 %all-reduce.8.cloned.1.call-start = ((), (), s32[]{:S(2)}) async-start(), calls=%async_computation.4 | async-start | bytes 8388608 | tf_op jit(solution)/shard_map/psum | solution.py:45
  423.0 6.6 %copy-start = (f32[1024,1024]{1,0:T(8,128)S(1)}, f32[1024,1024]{1,0:T(8,128)}, u32[]{:S(2)}) copy-start(f32[1024,1024]{1,0:T(8,128)} %all-reduce.6.cloned.1.call-done) | copy-start | bytes 12582916
  550.7 6.6 %copy-start.1 = (f32[1024,1024]{1,0:T(8,128)S(1)}, f32[1024,1024]{1,0:T(8,128)}, u32[]{:S(2)}) copy-start(f32[1024,1024]{1,0:T(8,128)} %all-reduce.8.cloned.1.call-done) | copy-start | bytes 12582916
Sparse Core Ops, SparseCore 0:
  27.9 111.9 reduce-scatter.1
  182.9 108.6 all-reduce.3
  311.6 111.3 all-reduce.5
  439.4 111.2 all-reduce.7
where the time goes:
time: 569 us
  waiting for transfers between devices  443 us (78%)
  matrix products  49.1 us (9%)
  blocking collectives  33.5 us (6%)
  other arithmetic  16.7 us (3%)
  between operations  15.2 us (3%)
  local copies, waits for them, and re-layouts  10.4 us (2%)
    psum x3, waiting for transfers between devices, body(): gram = lax.psum(partial_value, DP)  331 us
    reduce_scatter x1, waiting for transfers between devices, body(): lax.psum_scatter(local_grads[0, 0].astype(jnp.float32), DP, scatter_dimen...  112 us
    dot_general x9, matrix products, precise(): jnp.dot(left, right, precision=lax.Precision.HIGHEST, preferred_element_t...  49.1 us
    psum x4, blocking collectives, over_axes(): x = lax.psum(x, axis)  33.5 us
  transfers between devices with their start and end apart: 4, of which 4 were waited for; matrix products, arithmetic and copies ran while one was open for 0% of the time, Pallas kernels for 0%

commit v1 on v0

v1 whole, which is shorter than its diff:
```python
import math

import jax
import jax.numpy as jnp
from jax import lax
from jax.experimental import pallas as pl
from jax.experimental.pallas import tpu as pltpu
from jax.sharding import Mesh
from jax.sharding import PartitionSpec as P

MESH = pl.DeviceIdType.MESH
HID, WID = 1024, 3584
OWN = WID // 32
HALF = OWN // 2
LANES = HID // 2
ORDER = (2, 1, 3, 0)
DP = ("dp_0", "dp_1", "dp_2")
DP_EXPERT = DP + ("expert",)

first_coef = 3.4445
second_coef = -4.775
third_coef = 2.0315
momentum_decay = 0.95


def place():
    return [lax.axis_index(a) for a in ("dp_0", "dp_1", "dp_2", "expert")]


def reduce_scatter_kernel(x_hbm, out, raw, flat, mine, pa, pb, ra, rb, qa, qb, r2, load_sem, send_sem, recv_sem):
    y, z, c, x = place()
    partner = (y, z, 1 - c, x)
    y_next, y_prev = (lax.rem(y + 1, 4), z, c, x), (lax.rem(y + 3, 4), z, c, x)
    z_next, z_prev = (y, lax.rem(z + 1, 4), c, x), (y, lax.rem(z + 3, 4), c, x)
    loads = []
    for k in range(4):
        first = pl.multiple_of(lax.rem(y + ORDER[k], 4) * 896, 128)
        load = pltpu.make_async_copy(x_hbm.at[:, pl.ds(first, 896)], raw.at[k], load_sem.at[k])
        load.start()
        loads.append(load)
    barrier = pltpu.get_barrier_semaphore()
    for peer in (partner, y_next, y_prev, z_next, z_prev):
        pl.semaphore_signal(barrier, inc=1, device_id=peer, device_id_type=MESH)
    pl.semaphore_wait(barrier, 5)

    started = []

    def send(src, dst, peer):
        n = len(started)
        copy = pltpu.make_async_remote_copy(
            src_ref=src, dst_ref=dst, send_sem=send_sem.at[n], recv_sem=recv_sem.at[n],
            device_id=peer, device_id_type=MESH)
        copy.start()
        started.append(copy)
        return copy

    row = lax.broadcasted_iota(jnp.int32, (128, 128), 0)
    col = lax.broadcasted_iota(jnp.int32, (128, 128), 1)
    eye = jnp.where(row == col, 1.0, 0.0).astype(jnp.bfloat16)

    def turn(k):
        loads[k].wait()
        for b in range(7):
            flat[k, 128 * b:128 * b + 128, :] = lax.dot_general(
                eye, raw[k, :, 128 * b:128 * b + 128], (((1,), (1,)), ((), ())),
                preferred_element_type=jnp.float32)

    def rows_of(j, core):
        return pl.multiple_of((lax.rem(z + ORDER[j], 4) * 2 + core) * OWN, 8)

    pair = {}

    def exchange(k):
        for j in range(4):
            pair[k, j] = send(flat.at[k, pl.ds(rows_of(j, 1 - c), OWN)], mine.at[k, j], partner)

    def pair_sum(k):
        for j in range(4):
            pair[k, j].wait_recv()
            base = rows_of(j, c)
            for h in range(2):
                lanes = slice(LANES * h, LANES * h + LANES)
                pa[k, j, h] = flat[k, pl.ds(base, HALF), lanes] + mine[k, j, 0:HALF, lanes]
                pb[j, k, h] = flat[k, pl.ds(base + HALF, HALF), lanes] + mine[k, j, HALF:OWN, lanes]

    def relay(p, r, nxt, prv):
        return [send(p(0, 0), r.at[0], nxt), send(p(0, 1), r.at[1], prv)]

    def unmerged_next(p, r, nxt):
        return send(p(1, 1), r.at[2], nxt)

    def unmerged_prev(p, r, prv):
        return send(p(2, 0), r.at[3], prv)

    def merged(p, r, nxt, prv, relays):
        relays[0].wait_recv()
        p(1, 0)[...] += r[0]
        first = send(p(1, 0), r.at[4], nxt)
        relays[1].wait_recv()
        p(2, 1)[...] += r[1]
        return [first, send(p(2, 1), r.at[5], prv)]

    def total(p, r, parts):
        for part in parts:
            part.wait_recv()
        return p(3, 0)[...] + r[4] + r[3], p(3, 1)[...] + r[2] + r[5]

    a_slots = [lambda s, h, j=j: pa.at[s, j, h] for j in range(4)]
    b_slots = [lambda s, h, k=k: pb.at[s, k, h] for k in range(4)]
    a_sent, b_sent = [[] for _ in range(4)], [[] for _ in range(4)]
    a_relay, b_relay = [None] * 4, [None] * 4

    def launch(k):
        pair_sum(k)
        b_relay[k] = relay(b_slots[k], rb.at[k], z_next, z_prev)
        if k == 0:
            for j in range(4):
                a_relay[j] = relay(a_slots[j], ra.at[j], y_next, y_prev)
        b_sent[k] += [unmerged_next(b_slots[k], rb.at[k], z_next), unmerged_prev(b_slots[k], rb.at[k], z_prev)]
        if k == 1:
            for j in range(4):
                a_sent[j].append(unmerged_next(a_slots[j], ra.at[j], y_next))
        if k == 2:
            for j in range(4):
                a_sent[j].append(unmerged_prev(a_slots[j], ra.at[j], y_prev))

    turn(0)
    exchange(0)
    turn(1)
    exchange(1)
    launch(0)
    turn(2)
    exchange(2)
    launch(1)
    turn(3)
    exchange(3)
    launch(2)
    launch(3)
    for i in range(4):
        a_sent[i] += merged(a_slots[i], ra.at[i], y_next, y_prev, a_relay[i])
        b_sent[i] += merged(b_slots[i], rb.at[i], z_next, z_prev, b_relay[i])

    last_a, last_b = (lambda s, h: qa.at[s, h]), (lambda s, h: qb.at[s, h])
    a_last, b_last = [], []
    for i in range(4):
        for q, slots, r, sent in ((qa, a_slots, ra, a_sent), (qb, b_slots, rb, b_sent)):
            q[i, 0], q[i, 1] = total(slots[i], r.at[i], sent[i])
        for last, r, nxt, prv, kept in ((last_a, r2.at[0], z_next, z_prev, a_last), (last_b, r2.at[1], y_next, y_prev, b_last)):
            if i == 0:
                kept.append(relay(last, r, nxt, prv))
            if i == 1:
                kept.append(unmerged_next(last, r, nxt))
            if i == 2:
                kept.append(unmerged_prev(last, r, prv))
    a_last += merged(last_a, r2.at[0], z_next, z_prev, a_last[0])
    b_last += merged(last_b, r2.at[1], y_next, y_prev, b_last[0])
    out[0:HALF, 0:LANES], out[0:HALF, LANES:HID] = total(last_a, r2.at[0], a_last[1:])
    out[HALF:OWN, 0:LANES], out[HALF:OWN, LANES:HID] = total(last_b, r2.at[1], b_last[1:])
    for copy in started:
        copy.wait_send()


COPIES = 16 + 48 + 12


def reduce_scatter(local):
    piece = (HALF, LANES)
    return pl.pallas_call(
        reduce_scatter_kernel,
        out_shape=jax.ShapeDtypeStruct((OWN, HID), jnp.float32),
        in_specs=[pl.BlockSpec(memory_space=pl.ANY)],
        out_specs=pl.BlockSpec(memory_space=pltpu.VMEM),
        scratch_shapes=[
            pltpu.VMEM((4, HID, 896), jnp.bfloat16),
            pltpu.VMEM((4, 896, HID), jnp.float32),
            pltpu.VMEM((4, 4, OWN, HID), jnp.float32),
            pltpu.VMEM((4, 4, 2) + piece, jnp.float32),
            pltpu.VMEM((4, 4, 2) + piece, jnp.float32),
            pltpu.VMEM((4, 6) + piece, jnp.float32),
            pltpu.VMEM((4, 6) + piece, jnp.float32),
            pltpu.VMEM((4, 2) + piece, jnp.float32),
            pltpu.VMEM((4, 2) + piece, jnp.float32),
            pltpu.VMEM((2, 6) + piece, jnp.float32),
            pltpu.SemaphoreType.DMA((4,)),
            pltpu.SemaphoreType.DMA((COPIES,)),
            pltpu.SemaphoreType.DMA((COPIES,)),
        ],
        compiler_params=pltpu.CompilerParams(collective_id=0, has_side_effects=True, vmem_limit_bytes=60 << 20),
        name="sum_gradients",
    )(local)


def precise(left, right):
    return jnp.dot(left, right, precision=lax.Precision.HIGHEST, preferred_element_type=jnp.float32)


def body(local_grads, momentum):
    grads = reduce_scatter(local_grads[0, 0])
    total_sq = lax.psum(jnp.sum(grads * grads), DP_EXPERT)
    root_mean = jnp.sqrt(total_sq / (HID * WID * lax.axis_size("expert")) + 1e-06)
    clipped = jnp.minimum(1.0, 1.0 / root_mean) * grads
    new_momentum = momentum_decay * momentum[0].T + clipped
    blend = clipped + momentum_decay * new_momentum
    gram = lax.psum(precise(blend.T, blend), DP)
    norm = jnp.sqrt(jnp.trace(gram)) + 1e-07
    iterate = blend / norm
    gram = gram / (norm * norm)
    lower = second_coef * gram + third_coef * precise(gram, gram)
    left = first_coef * gram + precise(gram, lower)
    gram1 = first_coef * left + precise(left, lower)
    lower1 = second_coef * gram1 + third_coef * precise(gram1, gram1)

    def step1(value):
        return first_coef * value + precise(value, lower1)

    def gram2(value):
        return step1(precise(step1(value), gram1))

    iterate = step1(first_coef * iterate + precise(iterate, lower))
    product = gram2(iterate)
    iterate = first_coef * iterate + gram2(second_coef * iterate + third_coef * product)
    update = iterate * (0.2 * math.sqrt(max(HID, WID)))
    return (new_momentum.T[None], update.T[None])


def solution(mesh):
    finer = Mesh(mesh.devices.reshape(4, 4, 2, mesh.shape["expert"]), DP_EXPERT)
    in_specs = (P("expert", DP, None, None), P("expert", None, DP))
    out_specs = (P("expert", None, DP), P("expert", None, DP))
    return jax.shard_map(body, mesh=finer, in_specs=in_specs, out_specs=out_specs, check_vma=False)
```

time: 569 us -> 339 us (0.60)
  waiting for transfers between devices: 443 us -> 108 us
  Pallas kernels: 0 us -> 52.6 us
  matrix products: 49.1 us -> 88.3 us
  blocking collectives: 33.5 us -> 64.6 us
  other arithmetic: 16.7 us -> 5.5 us
  local copies, waits for them, and re-layouts: 10.4 us -> 0.01 us
    psum x3 -> x1, waiting for transfers between devices: 331 us -> 108 us  [body(): gram = lax.psum(precise(blend.T, blend), DP)]
    reduce_scatter x1 -> x0, waiting for transfers between devices: 112 us -> none  [body(): lax.psum_scatter(local_grads[0, 0].astype(jnp.float32), DP, scatter_dimen...]
    pallas_call x0 -> x1, Pallas kernels: none -> 52.6 us  [reduce_scatter(): pl.pallas_call(reduce_scatter_kernel, out_shape=jax.ShapeDtypeStruct((OWN...]
    dot_general x9 -> x13, matrix products: 49.1 us -> 88.3 us  [precise(): jnp.dot(left, right, precision=lax.Precision.HIGHEST, preferred_element_t...]
    psum x4 -> x1, blocking collectives: 33.5 us -> 64.6 us  [body(): total_sq = lax.psum(jnp.sum(grads * grads), DP_EXPERT)]
    unnamed x9 -> x6, local copies, waits for them, and re-layouts: 10.4 us -> 0.01 us
    convert_element_type x1 -> x0, other arithmetic: 10.2 us -> none  [body(): local_grads[0, 0].astype(jnp.float32)]
  transfers between devices with their start and end apart: 4 -> 1, of which waited for: 4 -> 1; matrix products, arithmetic and copies ran while one was open for 0% -> 0% of each run, Pallas kernels for 0% -> 0%
where the time goes in v1:
time: 339 us; the launch traced here: 334 us
  waiting for transfers between devices  108 us (32%)
  matrix products  88.3 us (26%)
  blocking collectives  64.6 us (19%)
  Pallas kernels  52.6 us (16%)
  between operations  15.7 us (5%)
  other arithmetic  5.5 us (2%)
    psum x1, waiting for transfers between devices, body(): gram = lax.psum(precise(blend.T, blend), DP)  108 us
    dot_general x13, matrix products, precise(): jnp.dot(left, right, precision=lax.Precision.HIGHEST, preferred_element_t...  88.3 us
    psum x1, blocking collectives, body(): total_sq = lax.psum(jnp.sum(grads * grads), DP_EXPERT)  64.6 us
    pallas_call x1, Pallas kernels, reduce_scatter(): pl.pallas_call(reduce_scatter_kernel, out_shape=jax.ShapeDtypeStruct((OWN...  52.6 us
  transfers between devices with their start and end apart: 1, of which 1 were waited for; matrix products, arithmetic and copies ran while one was open for 0% of the time, Pallas kernels for 0%

profile of v1, /device:TPU:1, one launch (start us, length us, event | category | flops | bytes accessed | tf_op | source)
XLA Modules:
  0.0 334.4 jit_solution(16193842281343329553)
XLA Ops:
  7.2 0.0 copy-start.2
  7.2 0.0 all-reduce.2.cloned.1.call-start
  7.2 52.6 %sum_gradients.1 = f32[112,1024]{1,0:T(8,128)} custom-call(bf16[1024,3584]{1,0:T(8,128)(2,1)} %bitcast.40), custom_call_target="tpu_custom_call" | custom-call | tf_op jit(solution)/shard_map/sum_gradients/pallas_call | solution.py:168
  59.8 1.7 multiply_reduce_fusion
  61.6 64.6 %psum.14 = f32[]{:T(128)} all-reduce(f32[]{:T(128)} %multiply_reduce_fusion), channel_id=1, replica_groups=mesh['dp_0'=4,'dp_1'=4,'dp_2'=2,'expert'=4] {'dp_0','dp_1','dp_2','expert'}, use_global_device_ids=true, to_apply=%region_1.0 | all-reduce | flops 1 | bytes 8 | tf_op jit(solution)/shard_map/psum | solution.py:199
  126.8 0.0 copy-done.2
  126.8 0.0 copy-start
  126.8 6.7 %fusion.28 = f32[1024,1024]{1,0:T(8,128)} fusion(f32[112,1024]{1,0:T(8,128)} %sum_gradients.1, f32[1,1024,112]{1,2,0:T(8,128)S(1)} %copy-done.2, f32[]{:T(128)S(6)} %min.3), kind=kOutput, calls=%fused_computation.41 | convolution fusion | flops 1409859584 | bytes 5111812 | tf_op jit(solution)/shard_map/dot_general | solution.py:194
  133.5 0.0 all-reduce.2.cloned.1.call-update
  133.5 0.0 copy-done
  133.5 0.8 fusion.25
  134.4 107.6 %all-reduce.2.cloned.1.call-done = f32[1024,1024]{1,0:T(8,128)} async-done(((f32[1024,1024]{1,0:T(8,128)}), f32[1024,1024]{1,0:T(8,128)}) %all-reduce.2.cloned.1.call-update) | async-done | bytes 4194320 | tf_op jit(solution)/shard_map/psum | solution.py:204
  242.0 2.9 select_reduce_fusion
  245.6 0.0 copy-start.1
  245.6 17.7 %fusion.38 = f32[1024,1024]{1,0:T(8,128)S(1)} fusion(f32[1024,1024]{1,0:T(8,128)} %all-reduce.2.cloned.1.call-done, f32[]{:T(128)S(6)} %mul.87), kind=kOutput, calls=%fused_computation.51 | convolution fusion | flops 12885950464 | bytes 8388612 | tf_op jit(solution)/shard_map/dot_general | solution.py:194
  263.4 0.0 copy-done.1
  263.4 14.0 %multiply_add_fusion.2 = f32[1024,1024]{1,0:T(8,128)S(1)} fusion(f32[1024,1024]{1,0:T(8,128)S(1)} %fusion.38, f32[1024,1024]{1,0:T(8,128)S(1)} %copy-done.1, f32[]{:T(128)S(6)} %mul.87), kind=kOutput, calls=%fused_computation.2 | convolution fusion | flops 12893290496 | bytes 12582916 | tf_op jit(solution)/shard_map/dot_general | solution.py:194
  277.4 14.3 %multiply_add_fusion.1 = f32[1024,1024]{1,0:T(8,128)S(1)} fusion(f32[1024,1024]{1,0:T(8,128)S(1)} %multiply_add_fusion.2, f32[1024,1024]{1,0:T(8,128)S(1)} %fusion.38, f32[1024,1024]{1,0:T(8,128)S(1)} %copy-done.1, f32[]{:T(128)S(6)} %mul.87), kind=kOutput, calls=%fused_computation.1 | convolution fusion | flops 12891193344 | bytes 16777220 | tf_op jit(solution)/shard_map/dot_general | solution.py:194
  291.7 14.3 %multiply_add_fusion = f32[1024,1024]{1,0:T(8,128)S(1)} fusion(f32[1024,1024]{1,0:T(8,128)S(1)} %multiply_add_fusion.1), kind=kOutput, calls=%fused_computation | convolution fusion | flops 12888047616 | bytes 8388608 | tf_op jit(solution)/shard_map/dot_general | solution.py:194
  306.1 3.4 %fusion.14 = f32[112,1024]{1,0:T(8,128)S(1)} fusion(f32[1024,1024]{1,0:T(8,128)S(1)} %fusion.38, f32[]{:T(128)S(6)} %add.55, f32[1,1024,112]{1,2,0:T(8,128)S(1)} %copy-done.2, f32[112,1024]{1,0:T(8,128)S(1)} %copy-done, f32[]{:T(128)S(6)} %min.3, f32[1024,1024]{1,0:T(8,128)S(1)} %copy-done.1, f32[]{:T(128)S(6)} %mul.87), kind=kOutput, calls=%fused_computation.23 | convolution fusion | flops 1415086080 | bytes 9764876 | tf_op jit(solution)/shard_map/dot_general | solution.py:194
  309.5 2.4 fusion.39
  311.9 2.4 fusion.20
  314.3 2.4 fusion.40
  316.7 2.5 fusion.16
  319.2 2.6 convolution_add_fusion.1
  321.8 2.4 fusion.41
  324.2 3.2 fusion.19
Async XLA Ops:
  7.2 119.7 %copy-start.2 = (f32[1,1024,112]{1,2,0:T(8,128)S(1)}, f32[1,1024,112]{1,2,0:T(8,128)}, u32[]{:S(2)}) copy-start(f32[1,1024,112]{1,2,0:T(8,128)} %param.3) | copy-start | bytes 1376260
  7.2 234.8 %all-reduce.2.cloned.1.call-start = ((), (), s32[]{:S(2)}) async-start(), calls=%async_computation | async-start | bytes 8388608 | tf_op jit(solution)/shard_map/psum | solution.py:204
  126.8 6.7 %copy-start = (f32[112,1024]{1,0:T(8,128)S(1)}, f32[112,1024]{1,0:T(8,128)}, u32[]{:S(2)}) copy-start(f32[112,1024]{1,0:T(8,128)} %sum_gradients.1) | copy-start | bytes 1376260
  245.6 17.7 %copy-start.1 = (f32[1024,1024]{1,0:T(8,128)S(1)}, f32[1024,1024]{1,0:T(8,128)}, u32[]{:S(2)}) copy-start(f32[1024,1024]{1,0:T(8,128)} %all-reduce.2.cloned.1.call-done) | copy-start | bytes 12582916
Sparse Core Ops, SparseCore 0:
  133.6 108.3 all-reduce.1

commit v2 on v1

--- a/solution.py
+++ b/solution.py
@@ -1,3 +1,4 @@
+import functools
 import math
 
 import jax
@@ -16,11 +17,6 @@
 ORDER = (2, 1, 3, 0)
 DP = ("dp_0", "dp_1", "dp_2")
 DP_EXPERT = DP + ("expert",)
-
-first_coef = 3.4445
-second_coef = -4.775
-third_coef = 2.0315
-momentum_decay = 0.95
 
 
 def place():
@@ -190,36 +186,317 @@
     )(local)
 
 
-def precise(left, right):
-    return jnp.dot(left, right, precision=lax.Precision.HIGHEST, preferred_element_type=jnp.float32)
+momentum_decay = 0.95
+BLOCK = 128
+PAIRS = (((0, 7), (3, 4)), ((1, 6), (2, 5)))
+FIRST = 5
+
+
+def halves(value):
+    high = value.astype(jnp.bfloat16)
+    return high, (value - high.astype(jnp.float32)).astype(jnp.bfloat16)
+
+
+def gram_kernel(count, g_ref, m_ref, new_ref, start_ref, gram_ref, s1, s2, s3, both, bb, a0, a1, b0, b1, r0, r1, q0, q1, t0, t1, w00, w01, w10, w11, send_sem, recv_sem):
+    y, z, c, x = place()
+    partner = (y, z, 1 - c, x)
+    line = x * 2 + c
+    y_line = [(lax.rem(y + d, 4), z, c, x) for d in (1, 2, 3)]
+    z_line = [(y, lax.rem(z + d, 4), c, x) for d in (1, 2, 3)]
+    x_line = [(y, z, lax.rem(lax.rem(line + d, 8), 2), lax.rem(line + d, 8) // 2) for d in range(1, 8)]
+    y_ring, z_ring = (y_line[0], y_line[2]), (z_line[0], z_line[2])
+    barrier = pltpu.get_barrier_semaphore()
+    for peer in x_line + y_line + z_line:
+        pl.semaphore_signal(barrier, inc=1, device_id=peer, device_id_type=MESH)
+    pl.semaphore_wait(barrier, 13)
+
+    started = []
+
+    def send(src, dst, peer):
+        n = len(started)
+        copy = pltpu.make_async_remote_copy(
+            src_ref=src, dst_ref=dst, send_sem=send_sem.at[n], recv_sem=recv_sem.at[n],
+            device_id=peer, device_id_type=MESH)
+        copy.start()
+        started.append(copy)
+        return copy
+
+    square = g_ref[0:8, :] * g_ref[0:8, :]
+    for i in range(1, OWN // 8):
+        square += g_ref[8 * i:8 * i + 8, :] * g_ref[8 * i:8 * i + 8, :]
+    tile = square[:, 0:128]
+    for i in range(1, 8):
+        tile += square[:, 128 * i:128 * i + 128]
+    for buf, own, peers in ((s1, line, x_line), (s2, y, y_line), (s3, z, z_line)):
+        buf[own] = tile
+        copies = [send(buf.at[own], buf.at[own], peer) for peer in peers]
+        if buf is s1:
+            pair = [send(g_ref, both.at[0], partner), send(m_ref, both.at[1], partner)]
+        for copy in copies:
+            copy.wait_recv()
+        tile = buf[0]
+        for i in range(1, buf.shape[0]):
+            tile += buf[i]
+    root_mean = jnp.sqrt(jnp.sum(tile, keepdims=True) / count + 1e-06)
+    factor = jnp.minimum(1.0, 1.0 / root_mean)
+    clipped = factor * g_ref[...]
+    new = momentum_decay * m_ref[...] + clipped
+    new_ref[...] = new
+    blend = clipped + momentum_decay * new
+    bb[0:OWN] = blend
+    for copy in pair:
+        copy.wait_recv()
+    clipped = factor * both[0]
+    bb[OWN:2 * OWN] = clipped + momentum_decay * (momentum_decay * both[1] + clipped)
+    high, low = halves(bb[...])
+    turned = bb[...].T
+    turned_high, turned_low = halves(turned)
+
+    def dot(left, right):
+        return jnp.dot(left, right, preferred_element_type=jnp.float32)
+
+    for core in range(2):
+        @pl.when(c == core)
+        def _(core=core):
+            for (first, second), (u0, u1) in zip(PAIRS[core], ((a0, a1), (b0, b1))):
+                swap = u0 is b0
+                place_in = 0
+                for b in (first, second):
+                    lh, ll = turned_high[BLOCK * b:BLOCK * b + BLOCK], turned_low[BLOCK * b:BLOCK * b + BLOCK]
+                    rh, rl = high[:, BLOCK * b:], low[:, BLOCK * b:]
+                    rows = dot(lh, rh) + (dot(lh, rl) + dot(ll, rh))
+                    for i in range(16):
+                        dy, dz = lax.rem(i // 4 + 4 - y, 4), lax.rem(i % 4 + 4 - z, 4)
+                        one, two = (dz, dy) if swap else (dy, dz)
+                        for t in range(8 - b):
+                            value = rows[8 * i:8 * i + 8, BLOCK * t:BLOCK * t + BLOCK]
+                            n = place_in + t
+                            if n < FIRST:
+                                u0[one, two, n] = value
+                            else:
+                                u1[one, two, n - FIRST] = value
+                    place_in += 8 - b
+
+    def begin(p, r, ring):
+        nxt, prv = ring
+        relays = [send(p[0].at[2], r[0].at[0], nxt), send(p[1].at[2], r[1].at[0], prv)]
+        return relays, [send(p[1].at[1], r[1].at[1], nxt), send(p[0].at[3], r[0].at[1], prv)]
+
+    def merge(p, r, ring, relays):
+        nxt, prv = ring
+        relays[0].wait_recv()
+        p[0][1] += r[0][0]
+        copies = [send(p[0].at[1], r[0].at[2], nxt)]
+        relays[1].wait_recv()
+        p[1][3] += r[1][0]
+        return copies + [send(p[1].at[3], r[1].at[2], prv)]
+
+    def end(p, r, copies):
+        for copy in copies:
+            copy.wait_recv()
+        return [p[h][0] + r[h][1] + r[h][2] for h in range(2)]
+
+    def at(refs, i):
+        return [ref.at[i] for ref in refs]
+
+    def reduce(sets):
+        begun = [begin(*s) for s in sets]
+        merged = [merge(*s, relays) + copies for s, (relays, copies) in zip(sets, begun)]
+        return [end(s[0], s[1], copies) for s, copies in zip(sets, merged)]
+
+    first_phase = reduce((((a0, a1), at((r0, r1), 0), y_ring), ((b0, b1), at((r0, r1), 1), z_ring)))
+    for i in range(2):
+        q0[i], q1[i] = first_phase[i]
+    second_phase = reduce(((at((q0, q1), 0), at((t0, t1), 0), z_ring), (at((q0, q1), 1), at((t0, t1), 1), y_ring)))
+
+    ws = ((w00.at[c], w01.at[c]), (w10.at[c], w11.at[c]))
+    for i in range(2):
+        ws[i][0][0, 0], ws[i][1][0, 0] = second_phase[i]
+
+    def gather(sets, seen):
+        stage = []
+        for p, (nxt, prv) in sets:
+            stage.append([
+                send(p[0].at[0], p[0].at[3], nxt), send(p[1].at[0], p[1].at[1], prv),
+                send(p[1].at[0], p[1].at[3], nxt), send(p[0].at[0], p[0].at[1], prv)])
+        relays = []
+        for n, (p, (nxt, prv)) in enumerate(sets):
+            stage[n][0].wait_recv()
+            relays.append(send(p[0].at[3], p[0].at[2], nxt))
+            stage[n][1].wait_recv()
+            relays.append(send(p[1].at[1], p[1].at[2], prv))
+            seen(n, (0, 3))
+            seen(n, (1, 1))
+        for n in range(2):
+            stage[n][2].wait_recv()
+            seen(n, (1, 3))
+            stage[n][3].wait_recv()
+            seen(n, (0, 1))
+        for n in range(2):
+            for h in range(2):
+                relays[2 * n + h].wait_recv()
+                seen(n, (h, 2))
+
+    gather(((at(ws[0], 0), z_ring), (at(ws[1], 0), y_ring)), lambda n, what: None)
+    other = []
+
+    def forward(n, what):
+        h, slot = what
+        other.append(send(ws[n][h].at[slot], ws[n][h].at[slot], partner))
+
+    for n in range(2):
+        for h in range(2):
+            forward(n, (h, 0))
+    gather(((ws[0], y_ring), (ws[1], z_ring)), forward)
+    for copy in other:
+        copy.wait_recv()
+
+    for core in range(2):
+        for (first, second), (u0, u1) in zip(PAIRS[core], ((w00, w01), (w10, w11))):
+            swap = u0 is w10
+            place_in = 0
+            for b in (first, second):
+                for i in range(16):
+                    dy, dz = lax.rem(i // 4 + 4 - y, 4), lax.rem(i % 4 + 4 - z, 4)
+                    one, two = (dz, dy) if swap else (dy, dz)
+                    for t in range(8 - b):
+                        n = place_in + t
+                        value = u0[core, one, two, n] if n < FIRST else u1[core, one, two, n - FIRST]
+                        gram_ref[BLOCK * b + 8 * i:BLOCK * b + 8 * i + 8, BLOCK * (b + t):BLOCK * (b + t + 1)] = value
+                place_in += 8 - b
+    row = lax.broadcasted_iota(jnp.int32, (BLOCK, BLOCK), 0)
+    col = lax.broadcasted_iota(jnp.int32, (BLOCK, BLOCK), 1)
+    diagonal = jnp.zeros((BLOCK, BLOCK), jnp.float32)
+    for b in range(8):
+        diagonal += jnp.where(row == col, gram_ref[BLOCK * b:BLOCK * b + BLOCK, BLOCK * b:BLOCK * b + BLOCK], 0.0)
+    norm = jnp.sqrt(jnp.sum(diagonal, keepdims=True)) + 1e-07
+    scale = 1.0 / norm
+    start_ref[...] = bb[0:OWN] * scale
+    square = scale * scale
+    for b in range(8):
+        for t in range(b, 8):
+            lanes = slice(BLOCK * t, BLOCK * t + BLOCK)
+            rows = slice(BLOCK * b, BLOCK * b + BLOCK)
+            value = gram_ref[rows, lanes] * square
+            gram_ref[rows, lanes] = value
+            if t > b:
+                gram_ref[lanes, rows] = value.T
+    for copy in started:
+        copy.wait_send()
+
+
+COPIES2 = 13 + 2 + 24 + 24 + 16
+
+
+def gram_of(grads, momentum, count):
+    part = ((FIRST, 8, BLOCK), (9 - FIRST, 8, BLOCK))
+    f32 = jnp.float32
+    both_parts = lambda *lead: [pltpu.VMEM(lead + p, f32) for p in part]
+    vmem = pl.BlockSpec(memory_space=pltpu.VMEM)
+    return pl.pallas_call(
+        functools.partial(gram_kernel, count),
+        out_shape=(jax.ShapeDtypeStruct((OWN, HID), f32), jax.ShapeDtypeStruct((OWN, HID), f32), jax.ShapeDtypeStruct((HID, HID), f32)),
+        in_specs=[vmem] * 2,
+        out_specs=[vmem] * 3,
+        scratch_shapes=[
+            pltpu.VMEM((8, 8, BLOCK), f32), pltpu.VMEM((4, 8, BLOCK), f32), pltpu.VMEM((4, 8, BLOCK), f32),
+            pltpu.VMEM((2, OWN, HID), f32), pltpu.VMEM((2 * OWN, HID), f32),
+            *both_parts(4, 4), *both_parts(4, 4),
+            *both_parts(2, 3, 4), *both_parts(2, 4), *both_parts(2, 3),
+            *both_parts(2, 4, 4), *both_parts(2, 4, 4),
+            pltpu.SemaphoreType.DMA((COPIES2,)), pltpu.SemaphoreType.DMA((COPIES2,)),
+        ],
+        compiler_params=pltpu.CompilerParams(collective_id=1, has_side_effects=True, vmem_limit_bytes=60 << 20),
+        name="reduce_gram",
+    )(grads, momentum)
+
+
+first_coef = 3.4445
+second_coef = -4.775
+third_coef = 2.0315
+TILE = 256
+
+
+def newton_schulz_kernel(gram_ref, start_ref, new_ref, out_ref, kept_ref, mats, left_ref, gram1_ref):
+    kept_ref[...] = new_ref[...]
+
+    def dot(left, right):
+        return jnp.dot(left, right, preferred_element_type=jnp.float32)
+
+    def keep(n, rows, lanes, value):
+        high, low = halves(value)
+        mats[n, 0, rows, lanes] = high
+        mats[n, 1, rows, lanes] = low
+
+    def cut(i):
+        return slice(TILE * i, TILE * i + TILE)
+
+    def product(left, right, new, base_ref, alpha, beta, new_ref):
+        for r in range(4):
+            high = mats[left, 0, cut(r), :]
+            both = jnp.concatenate([high, mats[left, 1, cut(r), :]], axis=0)
+            for q in range(r, 4):
+                value = dot(both, mats[right, 0, :, cut(q)])
+                value = value[:TILE] + (value[TILE:] + dot(high, mats[right, 1, :, cut(q)]))
+                value = alpha * base_ref[cut(r), cut(q)] + beta * value
+                keep(new, cut(r), cut(q), value)
+                if new_ref is not None:
+                    new_ref[cut(r), cut(q)] = value
+                if q > r:
+                    turned = value.T
+                    keep(new, cut(q), cut(r), turned)
+                    if new_ref is not None:
+                        new_ref[cut(q), cut(r)] = turned
+
+    def apply(value, n):
+        high, low = halves(value)
+        both = jnp.concatenate([high, low], axis=0)
+        parts = []
+        for q in range(4):
+            part = dot(both, mats[n, 0, :, cut(q)])
+            parts.append(part[:OWN] + (part[OWN:] + dot(high, mats[n, 1, :, cut(q)])))
+        return jnp.concatenate(parts, axis=1)
+
+    for i in range(4):
+        keep(0, cut(i), slice(None), gram_ref[cut(i), :])
+    product(0, 0, 1, gram_ref, second_coef, third_coef, None)
+    iterate = start_ref[...]
+    iterate = first_coef * iterate + apply(iterate, 1)
+    product(0, 1, 2, gram_ref, first_coef, 1.0, left_ref)
+    product(2, 1, 3, left_ref, first_coef, 1.0, gram1_ref)
+    product(3, 3, 4, gram1_ref, second_coef, third_coef, None)
+
+    def step1(value):
+        return first_coef * value + apply(value, 4)
+
+    def gram2(value):
+        return step1(apply(step1(value), 3))
+
+    iterate = step1(iterate)
+    twice = second_coef * iterate + third_coef * gram2(iterate)
+    iterate = first_coef * iterate + gram2(twice)
+    out_ref[...] = iterate * (0.2 * math.sqrt(max(HID, WID)))
+
+
+def newton_schulz(gram, start, new_momentum):
+    f32 = jnp.float32
+    vmem = pl.BlockSpec(memory_space=pltpu.VMEM)
+    return pl.pallas_call(
+        newton_schulz_kernel,
+        out_shape=[jax.ShapeDtypeStruct((OWN, HID), f32)] * 2,
+        in_specs=[vmem] * 3,
+        out_specs=[vmem] * 2,
+        scratch_shapes=[pltpu.VMEM((5, 2, HID, HID), jnp.bfloat16), pltpu.VMEM((HID, HID), f32), pltpu.VMEM((HID, HID), f32)],
+        compiler_params=pltpu.CompilerParams(vmem_limit_bytes=60 << 20),
+        name="newton_schulz",
+    )(gram, start, new_momentum)
 
 
 def body(local_grads, momentum):
     grads = reduce_scatter(local_grads[0, 0])
-    total_sq = lax.psum(jnp.sum(grads * grads), DP_EXPERT)
-    root_mean = jnp.sqrt(total_sq / (HID * WID * lax.axis_size("expert")) + 1e-06)
-    clipped = jnp.minimum(1.0, 1.0 / root_mean) * grads
-    new_momentum = momentum_decay * momentum[0].T + clipped
-    blend = clipped + momentum_decay * new_momentum
-    gram = lax.psum(precise(blend.T, blend), DP)
-    norm = jnp.sqrt(jnp.trace(gram)) + 1e-07
-    iterate = blend / norm
-    gram = gram / (norm * norm)
-    lower = second_coef * gram + third_coef * precise(gram, gram)
-    left = first_coef * gram + precise(gram, lower)
-    gram1 = first_coef * left + precise(left, lower)
-    lower1 = second_coef * gram1 + third_coef * precise(gram1, gram1)
-
-    def step1(value):
-        return first_coef * value + precise(value, lower1)
-
-    def gram2(value):
-        return step1(precise(step1(value), gram1))
-
-    iterate = step1(first_coef * iterate + precise(iterate, lower))
-    product = gram2(iterate)
-    iterate = first_coef * iterate + gram2(second_coef * iterate + third_coef * product)
-    update = iterate * (0.2 * math.sqrt(max(HID, WID)))
+    count = HID * WID * lax.axis_size("expert")
+    new_momentum, start, gram = gram_of(grads, momentum[0].T, count)
+    update, new_momentum = newton_schulz(gram, start, new_momentum)
     return (new_momentum.T[None], update.T[None])
 
 

time: 339 us -> 133 us (0.39); the launches traced: 334 us -> 133 us
  waiting for transfers between devices: 108 us -> 0 us
  matrix products: 88.3 us -> 0 us
  Pallas kernels: 52.6 us -> 132 us
  blocking collectives: 64.6 us -> 0 us
  between operations: 15.7 us -> 0.65 us
  other arithmetic: 5.5 us -> 0 us
    psum x1 -> x0, waiting for transfers between devices: 108 us -> none  [body(): gram = lax.psum(precise(blend.T, blend), DP)]
    dot_general x13 -> x0, matrix products: 88.3 us -> none  [precise(): jnp.dot(left, right, precision=lax.Precision.HIGHEST, preferred_element_t...]
    pallas_call x0 -> x2, Pallas kernels: none -> 79.3 us  [the longest x1 53.3 us: gram_of(): pl.pallas_call(functools.partial(gram_kernel, count), out_shape=(jax.Shap...]
    psum x1 -> x0, blocking collectives: 64.6 us -> none  [body(): total_sq = lax.psum(jnp.sum(grads * grads), DP_EXPERT)]
    reduce_sum x2 -> x0, other arithmetic: 4.67 us -> none  [the longest x1 2.93 us: body(): norm = jnp.sqrt(jnp.trace(gram)) + 1e-07]
  transfers between devices with their start and end apart: 1 -> 0, of which waited for: 1 -> 0; matrix products, arithmetic and copies ran while one was open for 0% -> 0% of each run, Pallas kernels for 0% -> 0%
where the time goes in v2:
time: 133 us
  Pallas kernels  132 us (99%)
    pallas_call x1, Pallas kernels, gram_of(): pl.pallas_call(functools.partial(gram_kernel, count), out_shape=(jax.Shap...  53.3 us
    pallas_call x1, Pallas kernels, reduce_scatter(): pl.pallas_call(reduce_scatter_kernel, out_shape=jax.ShapeDtypeStruct((OWN...  52.5 us
    pallas_call x1, Pallas kernels, newton_schulz(): pl.pallas_call(newton_schulz_kernel, out_shape=[jax.ShapeDtypeStruct((OWN...  26 us

profile of v2, /device:TPU:1, one launch (start us, length us, event | category | flops | bytes accessed | tf_op | source)
XLA Modules:
  0.0 132.5 jit_solution(2652888472270603709)
XLA Ops:
  0.6 52.5 %sum_gradients.1.g_ref = f32[112,1024]{1,0:T(8,128)} custom-call(bf16[1024,3584]{1,0:T(8,128)(2,1)} %bitcast.10), custom_call_target="tpu_custom_call" | custom-call | tf_op jit(solution)/shard_map/sum_gradients/pallas_call | solution.py:164
  53.2 53.3 %reduce_gram.1 = (f32[112,1024]{1,0:T(8,128)}, f32[112,1024]{1,0:T(8,128)}, f32[1024,1024]{1,0:T(8,128)}) custom-call(f32[112,1024]{1,0:T(8,128)} %sum_gradients.1.g_ref, f32[112,1024]{1,0:T(8,128)} %bitcast.11), custom_call_target="tpu_custom_call" | custom-call | tf_op jit(solution)/shard_map/reduce_gram/pallas_call | solution.py:396
  106.5 26.0 %newton_schulz.1 = (f32[112,1024]{1,0:T(8,128)}, f32[112,1024]{1,0:T(8,128)}) custom-call(f32[1024,1024]{1,0:T(8,128)} %get-tuple-element.7.gram_ref, f32[112,1024]{1,0:T(8,128)} %get-tuple-element.8.start_ref, f32[112,1024]{1,0:T(8,128)} %get-tuple-element.9.new_ref), custom_call_target="tpu_custom_call" | custom-call | tf_op jit(solution)/shard_map/newton_schulz/pallas_call | solution.py:484

commit v3 on v2

--- a/solution.py
+++ b/solution.py
@@ -19,11 +19,23 @@
 DP_EXPERT = DP + ("expert",)
 
 
+momentum_decay = 0.95
+BLOCK = 128
+PAIRS = (((0, 7), (3, 4)), ((1, 6), (2, 5)))
+FIRST = 5
+COPIES = 76 + 22 + 2 + 60 + 60 + 16
+
+
+def halves(value):
+    high = value.astype(jnp.bfloat16)
+    return high, (value - high.astype(jnp.float32)).astype(jnp.bfloat16)
+
+
 def place():
     return [lax.axis_index(a) for a in ("dp_0", "dp_1", "dp_2", "expert")]
 
 
-def reduce_scatter_kernel(x_hbm, out, raw, flat, mine, pa, pb, ra, rb, qa, qb, r2, load_sem, send_sem, recv_sem):
+def gram_kernel(count, x_hbm, m_hbm, new_ref, start_ref, gram_ref, raw, flat, mine, pa, pb, ra, rb, qa, qb, r2, both_g, both_m, s1, s2, bb, a0, a1, b0, b1, r0, r1, q0, q1, t0, t1, w00, w01, w10, w11, load_sem, send_sem, recv_sem):
     y, z, c, x = place()
     partner = (y, z, 1 - c, x)
     y_next, y_prev = (lax.rem(y + 1, 4), z, c, x), (lax.rem(y + 3, 4), z, c, x)
@@ -34,10 +46,16 @@
         load = pltpu.make_async_copy(x_hbm.at[:, pl.ds(first, 896)], raw.at[k], load_sem.at[k])
         load.start()
         loads.append(load)
+    load = pltpu.make_async_copy(m_hbm, both_m.at[0], load_sem.at[4])
+    load.start()
+    loads.append(load)
+    line = x * 2 + c
+    x_line = [(y, z, lax.rem(lax.rem(line + d, 8), 2), lax.rem(line + d, 8) // 2) for d in range(1, 8)]
+    spot = y * 4 + z
+    plane = [(lax.rem(spot + d, 16) // 4, lax.rem(lax.rem(spot + d, 16), 4), c, x) for d in range(1, 16)]
     barrier = pltpu.get_barrier_semaphore()
-    for peer in (partner, y_next, y_prev, z_next, z_prev):
+    for peer in x_line + plane:
         pl.semaphore_signal(barrier, inc=1, device_id=peer, device_id_type=MESH)
-    pl.semaphore_wait(barrier, 5)
 
     started = []
 
@@ -121,9 +139,12 @@
                 a_sent[j].append(unmerged_prev(a_slots[j], ra.at[j], y_prev))
 
     turn(0)
+    pl.semaphore_wait(barrier, 22)
     exchange(0)
     turn(1)
     exchange(1)
+    loads[4].wait()
+    pair_m = send(both_m.at[0], both_m.at[1], partner)
     launch(0)
     turn(2)
     exchange(2)
@@ -150,88 +171,20 @@
                 kept.append(unmerged_prev(last, r, prv))
     a_last += merged(last_a, r2.at[0], z_next, z_prev, a_last[0])
     b_last += merged(last_b, r2.at[1], y_next, y_prev, b_last[0])
+    out = both_g.at[0]
     out[0:HALF, 0:LANES], out[0:HALF, LANES:HID] = total(last_a, r2.at[0], a_last[1:])
     out[HALF:OWN, 0:LANES], out[HALF:OWN, LANES:HID] = total(last_b, r2.at[1], b_last[1:])
-    for copy in started:
-        copy.wait_send()
-
-
-COPIES = 16 + 48 + 12
-
-
-def reduce_scatter(local):
-    piece = (HALF, LANES)
-    return pl.pallas_call(
-        reduce_scatter_kernel,
-        out_shape=jax.ShapeDtypeStruct((OWN, HID), jnp.float32),
-        in_specs=[pl.BlockSpec(memory_space=pl.ANY)],
-        out_specs=pl.BlockSpec(memory_space=pltpu.VMEM),
-        scratch_shapes=[
-            pltpu.VMEM((4, HID, 896), jnp.bfloat16),
-            pltpu.VMEM((4, 896, HID), jnp.float32),
-            pltpu.VMEM((4, 4, OWN, HID), jnp.float32),
-            pltpu.VMEM((4, 4, 2) + piece, jnp.float32),
-            pltpu.VMEM((4, 4, 2) + piece, jnp.float32),
-            pltpu.VMEM((4, 6) + piece, jnp.float32),
-            pltpu.VMEM((4, 6) + piece, jnp.float32),
-            pltpu.VMEM((4, 2) + piece, jnp.float32),
-            pltpu.VMEM((4, 2) + piece, jnp.float32),
-            pltpu.VMEM((2, 6) + piece, jnp.float32),
-            pltpu.SemaphoreType.DMA((4,)),
-            pltpu.SemaphoreType.DMA((COPIES,)),
-            pltpu.SemaphoreType.DMA((COPIES,)),
-        ],
-        compiler_params=pltpu.CompilerParams(collective_id=0, has_side_effects=True, vmem_limit_bytes=60 << 20),
-        name="sum_gradients",
-    )(local)
-
-
-momentum_decay = 0.95
-BLOCK = 128
-PAIRS = (((0, 7), (3, 4)), ((1, 6), (2, 5)))
-FIRST = 5
-
-
-def halves(value):
-    high = value.astype(jnp.bfloat16)
-    return high, (value - high.astype(jnp.float32)).astype(jnp.bfloat16)
-
-
-def gram_kernel(count, g_ref, m_ref, new_ref, start_ref, gram_ref, s1, s2, s3, both, bb, a0, a1, b0, b1, r0, r1, q0, q1, t0, t1, w00, w01, w10, w11, send_sem, recv_sem):
-    y, z, c, x = place()
-    partner = (y, z, 1 - c, x)
-    line = x * 2 + c
-    y_line = [(lax.rem(y + d, 4), z, c, x) for d in (1, 2, 3)]
-    z_line = [(y, lax.rem(z + d, 4), c, x) for d in (1, 2, 3)]
-    x_line = [(y, z, lax.rem(lax.rem(line + d, 8), 2), lax.rem(line + d, 8) // 2) for d in range(1, 8)]
-    y_ring, z_ring = (y_line[0], y_line[2]), (z_line[0], z_line[2])
-    barrier = pltpu.get_barrier_semaphore()
-    for peer in x_line + y_line + z_line:
-        pl.semaphore_signal(barrier, inc=1, device_id=peer, device_id_type=MESH)
-    pl.semaphore_wait(barrier, 13)
-
-    started = []
-
-    def send(src, dst, peer):
-        n = len(started)
-        copy = pltpu.make_async_remote_copy(
-            src_ref=src, dst_ref=dst, send_sem=send_sem.at[n], recv_sem=recv_sem.at[n],
-            device_id=peer, device_id_type=MESH)
-        copy.start()
-        started.append(copy)
-        return copy
-
-    square = g_ref[0:8, :] * g_ref[0:8, :]
+    square = out[0:8, :] * out[0:8, :]
     for i in range(1, OWN // 8):
-        square += g_ref[8 * i:8 * i + 8, :] * g_ref[8 * i:8 * i + 8, :]
+        square += out[8 * i:8 * i + 8, :] * out[8 * i:8 * i + 8, :]
     tile = square[:, 0:128]
     for i in range(1, 8):
         tile += square[:, 128 * i:128 * i + 128]
-    for buf, own, peers in ((s1, line, x_line), (s2, y, y_line), (s3, z, z_line)):
+    for buf, own, peers in ((s1, line, x_line), (s2, spot, plane)):
         buf[own] = tile
         copies = [send(buf.at[own], buf.at[own], peer) for peer in peers]
         if buf is s1:
-            pair = [send(g_ref, both.at[0], partner), send(m_ref, both.at[1], partner)]
+            pair_g = send(out, both_g.at[1], partner)
         for copy in copies:
             copy.wait_recv()
         tile = buf[0]
@@ -239,15 +192,15 @@
             tile += buf[i]
     root_mean = jnp.sqrt(jnp.sum(tile, keepdims=True) / count + 1e-06)
     factor = jnp.minimum(1.0, 1.0 / root_mean)
-    clipped = factor * g_ref[...]
-    new = momentum_decay * m_ref[...] + clipped
+    clipped = factor * out[...]
+    new = momentum_decay * both_m[0] + clipped
     new_ref[...] = new
     blend = clipped + momentum_decay * new
     bb[0:OWN] = blend
-    for copy in pair:
-        copy.wait_recv()
-    clipped = factor * both[0]
-    bb[OWN:2 * OWN] = clipped + momentum_decay * (momentum_decay * both[1] + clipped)
+    pair_g.wait_recv()
+    pair_m.wait_recv()
+    clipped = factor * both_g[1]
+    bb[OWN:2 * OWN] = clipped + momentum_decay * (momentum_decay * both_m[1] + clipped)
     high, low = halves(bb[...])
     turned = bb[...].T
     turned_high, turned_low = halves(turned)
@@ -277,77 +230,87 @@
                                 u1[one, two, n - FIRST] = value
                     place_in += 8 - b
 
-    def begin(p, r, ring):
-        nxt, prv = ring
-        relays = [send(p[0].at[2], r[0].at[0], nxt), send(p[1].at[2], r[1].at[0], prv)]
-        return relays, [send(p[1].at[1], r[1].at[1], nxt), send(p[0].at[3], r[0].at[1], prv)]
-
-    def merge(p, r, ring, relays):
-        nxt, prv = ring
-        relays[0].wait_recv()
-        p[0][1] += r[0][0]
-        copies = [send(p[0].at[1], r[0].at[2], nxt)]
-        relays[1].wait_recv()
-        p[1][3] += r[1][0]
-        return copies + [send(p[1].at[3], r[1].at[2], prv)]
-
-    def end(p, r, copies):
-        for copy in copies:
+    y_far, z_far = (lax.rem(y + 2, 4), z, c, x), (y, lax.rem(z + 2, 4), c, x)
+    y_ring, z_ring = {1: y_next, 2: y_far, 3: y_prev}, {1: z_next, 2: z_far, 3: z_prev}
+    colours = ((0, (a0, a1), y_ring, z_ring), (1, (b0, b1), z_ring, y_ring))
+    far_first = (2, 1, 3, 0)
+    relays, parts, lasts = {}, {}, [[], []]
+    for s in far_first:
+        for n, p, ring, _ in colours:
+            relays[n, s] = [send(p[0].at[2, s], r0.at[n, 0, s], ring[1]), send(p[1].at[2, s], r1.at[n, 0, s], ring[3])]
+    for s in far_first:
+        for n, p, ring, _ in colours:
+            parts[n, s] = [send(p[1].at[1, s], r1.at[n, 1, s], ring[1]), send(p[0].at[3, s], r0.at[n, 1, s], ring[3])]
+    for s in far_first:
+        for n, p, ring, _ in colours:
+            relays[n, s][0].wait_recv()
+            p[0][1, s] += r0[n, 0, s]
+            parts[n, s].append(send(p[0].at[1, s], r0.at[n, 2, s], ring[1]))
+            relays[n, s][1].wait_recv()
+            p[1][3, s] += r1[n, 0, s]
+            parts[n, s].append(send(p[1].at[3, s], r1.at[n, 2, s], ring[3]))
+    for s in far_first:
+        for n, p, _, ring in colours:
+            for copy in parts[n, s]:
+                copy.wait_recv()
+            q0[n, s] = p[0][0, s] + r0[n, 1, s] + r0[n, 2, s]
+            q1[n, s] = p[1][0, s] + r1[n, 1, s] + r1[n, 2, s]
+            if s > 0:
+                lasts[n] += [send(q0.at[n, s], t0.at[n, s], ring[s]), send(q1.at[n, s], t1.at[n, s], ring[s])]
+
+    ws = ((w00.at[c], w01.at[c]), (w10.at[c], w11.at[c]))
+    came, ring_parts, ring_relays, other = {}, {}, {}, []
+    for n, _, _, ring in colours:
+        for copy in lasts[n]:
             copy.wait_recv()
-        return [p[h][0] + r[h][1] + r[h][2] for h in range(2)]
-
-    def at(refs, i):
-        return [ref.at[i] for ref in refs]
-
-    def reduce(sets):
-        begun = [begin(*s) for s in sets]
-        merged = [merge(*s, relays) + copies for s, (relays, copies) in zip(sets, begun)]
-        return [end(s[0], s[1], copies) for s, copies in zip(sets, merged)]
-
-    first_phase = reduce((((a0, a1), at((r0, r1), 0), y_ring), ((b0, b1), at((r0, r1), 1), z_ring)))
-    for i in range(2):
-        q0[i], q1[i] = first_phase[i]
-    second_phase = reduce(((at((q0, q1), 0), at((t0, t1), 0), z_ring), (at((q0, q1), 1), at((t0, t1), 1), y_ring)))
-
-    ws = ((w00.at[c], w01.at[c]), (w10.at[c], w11.at[c]))
-    for i in range(2):
-        ws[i][0][0, 0], ws[i][1][0, 0] = second_phase[i]
-
-    def gather(sets, seen):
-        stage = []
-        for p, (nxt, prv) in sets:
-            stage.append([
-                send(p[0].at[0], p[0].at[3], nxt), send(p[1].at[0], p[1].at[1], prv),
-                send(p[1].at[0], p[1].at[3], nxt), send(p[0].at[0], p[0].at[1], prv)])
-        relays = []
-        for n, (p, (nxt, prv)) in enumerate(sets):
-            stage[n][0].wait_recv()
-            relays.append(send(p[0].at[3], p[0].at[2], nxt))
-            stage[n][1].wait_recv()
-            relays.append(send(p[1].at[1], p[1].at[2], prv))
-            seen(n, (0, 3))
-            seen(n, (1, 1))
+        ws[n][0][0, 0] = q0[n, 0] + t0[n, 1] + t0[n, 2] + t0[n, 3]
+        ws[n][1][0, 0] = q1[n, 0] + t1[n, 1] + t1[n, 2] + t1[n, 3]
+        for d in (2, 1, 3):
+            came[n, 4 - d] = [send(w.at[0, 0], w.at[0, 4 - d], ring[d]) for w in ws[n]]
+
+    def around(n, s):
+        ring, (u0, u1) = colours[n][2], ws[n]
+        ring_parts[n, s] = [
+            send(u0.at[0, s], u0.at[3, s], ring[1]), send(u1.at[0, s], u1.at[1, s], ring[3]),
+            send(u1.at[0, s], u1.at[3, s], ring[1]), send(u0.at[0, s], u0.at[1, s], ring[3])]
+
+    def pass_on(n, s):
+        ring, (u0, u1) = colours[n][2], ws[n]
+        ring_parts[n, s][0].wait_recv()
+        first = send(u0.at[3, s], u0.at[2, s], ring[1])
+        ring_parts[n, s][1].wait_recv()
+        ring_relays[n, s] = [first, send(u1.at[1, s], u1.at[2, s], ring[3])]
+
+    def forward(n, slot):
+        for w in ws[n]:
+            other.append(send(w.at[slot], w.at[slot], partner))
+
+    for n in range(2):
+        around(n, 0)
+    for s in (1, 3, 2):
         for n in range(2):
-            stage[n][2].wait_recv()
-            seen(n, (1, 3))
-            stage[n][3].wait_recv()
-            seen(n, (0, 1))
+            for copy in came[n, s]:
+                copy.wait_recv()
+            around(n, s)
+        if s == 3:
+            for n in range(2):
+                pass_on(n, 0)
+    for n in range(2):
+        forward(n, 0)
+    for s in (1, 3, 2):
         for n in range(2):
-            for h in range(2):
-                relays[2 * n + h].wait_recv()
-                seen(n, (h, 2))
-
-    gather(((at(ws[0], 0), z_ring), (at(ws[1], 0), y_ring)), lambda n, what: None)
-    other = []
-
-    def forward(n, what):
-        h, slot = what
-        other.append(send(ws[n][h].at[slot], ws[n][h].at[slot], partner))
-
+            pass_on(n, s)
     for n in range(2):
-        for h in range(2):
-            forward(n, (h, 0))
-    gather(((ws[0], y_ring), (ws[1], z_ring)), forward)
+        for s in range(4):
+            ring_parts[n, s][2].wait_recv()
+            ring_parts[n, s][3].wait_recv()
+        forward(n, 1)
+        forward(n, 3)
+    for n in range(2):
+        for s in range(4):
+            for copy in ring_relays[n, s]:
+                copy.wait_recv()
+        forward(n, 2)
     for copy in other:
         copy.wait_recv()
 
@@ -385,30 +348,39 @@
         copy.wait_send()
 
 
-COPIES2 = 13 + 2 + 24 + 24 + 16
-
-
-def gram_of(grads, momentum, count):
-    part = ((FIRST, 8, BLOCK), (9 - FIRST, 8, BLOCK))
+def gram_of(local, momentum, count):
     f32 = jnp.float32
-    both_parts = lambda *lead: [pltpu.VMEM(lead + p, f32) for p in part]
+    piece = (HALF, LANES)
+    cut = ((FIRST, 8, BLOCK), (9 - FIRST, 8, BLOCK))
+
+    def scratch(*lead):
+        return [pltpu.VMEM(lead + p, f32) for p in cut]
+
     vmem = pl.BlockSpec(memory_space=pltpu.VMEM)
     return pl.pallas_call(
         functools.partial(gram_kernel, count),
         out_shape=(jax.ShapeDtypeStruct((OWN, HID), f32), jax.ShapeDtypeStruct((OWN, HID), f32), jax.ShapeDtypeStruct((HID, HID), f32)),
-        in_specs=[vmem] * 2,
+        in_specs=[pl.BlockSpec(memory_space=pl.ANY)] * 2,
         out_specs=[vmem] * 3,
         scratch_shapes=[
-            pltpu.VMEM((8, 8, BLOCK), f32), pltpu.VMEM((4, 8, BLOCK), f32), pltpu.VMEM((4, 8, BLOCK), f32),
-            pltpu.VMEM((2, OWN, HID), f32), pltpu.VMEM((2 * OWN, HID), f32),
-            *both_parts(4, 4), *both_parts(4, 4),
-            *both_parts(2, 3, 4), *both_parts(2, 4), *both_parts(2, 3),
-            *both_parts(2, 4, 4), *both_parts(2, 4, 4),
-            pltpu.SemaphoreType.DMA((COPIES2,)), pltpu.SemaphoreType.DMA((COPIES2,)),
+            pltpu.VMEM((4, HID, 896), jnp.bfloat16),
+            pltpu.VMEM((4, 896, HID), f32),
+            pltpu.VMEM((4, 4, OWN, HID), f32),
+            pltpu.VMEM((4, 4, 2) + piece, f32), pltpu.VMEM((4, 4, 2) + piece, f32),
+            pltpu.VMEM((4, 6) + piece, f32), pltpu.VMEM((4, 6) + piece, f32),
+            pltpu.VMEM((4, 2) + piece, f32), pltpu.VMEM((4, 2) + piece, f32),
+            pltpu.VMEM((2, 6) + piece, f32),
+            pltpu.VMEM((2, OWN, HID), f32), pltpu.VMEM((2, OWN, HID), f32),
+            pltpu.VMEM((8, 8, BLOCK), f32), pltpu.VMEM((16, 8, BLOCK), f32),
+            pltpu.VMEM((2 * OWN, HID), f32),
+            *scratch(4, 4), *scratch(4, 4), *scratch(2, 3, 4), *scratch(2, 4), *scratch(2, 4),
+            *scratch(2, 4, 4), *scratch(2, 4, 4),
+            pltpu.SemaphoreType.DMA((5,)),
+            pltpu.SemaphoreType.DMA((COPIES,)), pltpu.SemaphoreType.DMA((COPIES,)),
         ],
-        compiler_params=pltpu.CompilerParams(collective_id=1, has_side_effects=True, vmem_limit_bytes=60 << 20),
-        name="reduce_gram",
-    )(grads, momentum)
+        compiler_params=pltpu.CompilerParams(collective_id=0, has_side_effects=True, vmem_limit_bytes=63 << 20),
+        name="gram_of_sum",
+    )(local, momentum)
 
 
 first_coef = 3.4445
@@ -493,9 +465,8 @@
 
 
 def body(local_grads, momentum):
-    grads = reduce_scatter(local_grads[0, 0])
     count = HID * WID * lax.axis_size("expert")
-    new_momentum, start, gram = gram_of(grads, momentum[0].T, count)
+    new_momentum, start, gram = gram_of(local_grads[0, 0], momentum[0].T, count)
     update, new_momentum = newton_schulz(gram, start, new_momentum)
     return (new_momentum.T[None], update.T[None])
 

time: 133 us -> 121 us (0.910)
  Pallas kernels: 132 us -> 120 us
    pallas_call x1 -> x0, Pallas kernels: 52.5 us -> none  [reduce_scatter(): pl.pallas_call(reduce_scatter_kernel, out_shape=jax.ShapeDtypeStruct((OWN...]
    pallas_call x1, Pallas kernels: 53.3 us -> 94.5 us  [gram_of(): pl.pallas_call(functools.partial(gram_kernel, count), out_shape=(jax.Shap...]
where the time goes in v3:
time: 121 us
  Pallas kernels  120 us (99%)
    pallas_call x1, Pallas kernels, gram_of(): pl.pallas_call(functools.partial(gram_kernel, count), out_shape=(jax.Shap...  94.5 us
    pallas_call x1, Pallas kernels, newton_schulz(): pl.pallas_call(newton_schulz_kernel, out_shape=[jax.ShapeDtypeStruct((OWN...  26 us

profile of v3, /device:TPU:1, one launch (start us, length us, event | category | flops | bytes accessed | tf_op | source)
XLA Modules:
  0.0 121.1 jit_solution(9502170270323828084)
XLA Ops:
  0.6 94.5 %gram_of_sum.1 = (f32[112,1024]{1,0:T(8,128)}, f32[112,1024]{1,0:T(8,128)}, f32[1024,1024]{1,0:T(8,128)}) custom-call(bf16[1024,3584]{1,0:T(8,128)(2,1)} %bitcast.10, f32[112,1024]{1,0:T(8,128)} %bitcast.11), custom_call_target="tpu_custom_call" | custom-call | tf_op jit(solution)/shard_map/gram_of_sum/pallas_call | solution.py:360
  95.1 26.0 %newton_schulz.1 = (f32[112,1024]{1,0:T(8,128)}, f32[112,1024]{1,0:T(8,128)}) custom-call(f32[1024,1024]{1,0:T(8,128)} %get-tuple-element.7.gram_ref, f32[112,1024]{1,0:T(8,128)} %get-tuple-element.8.start_ref, f32[112,1024]{1,0:T(8,128)} %get-tuple-element.9.new_ref), custom_call_target="tpu_custom_call" | custom-call | tf_op jit(solution)/shard_map/newton_schulz/pallas_call | solution.py:456

commit v4 on v3

--- a/solution.py
+++ b/solution.py
@@ -23,7 +23,7 @@
 BLOCK = 128
 PAIRS = (((0, 7), (3, 4)), ((1, 6), (2, 5)))
 FIRST = 5
-COPIES = 76 + 22 + 2 + 60 + 60 + 16
+COPIES = 76 + 22 + 2 + 60 + 60 + 64
 
 
 def halves(value):
@@ -88,14 +88,13 @@
         for j in range(4):
             pair[k, j] = send(flat.at[k, pl.ds(rows_of(j, 1 - c), OWN)], mine.at[k, j], partner)
 
-    def pair_sum(k):
-        for j in range(4):
-            pair[k, j].wait_recv()
-            base = rows_of(j, c)
-            for h in range(2):
-                lanes = slice(LANES * h, LANES * h + LANES)
-                pa[k, j, h] = flat[k, pl.ds(base, HALF), lanes] + mine[k, j, 0:HALF, lanes]
-                pb[j, k, h] = flat[k, pl.ds(base + HALF, HALF), lanes] + mine[k, j, HALF:OWN, lanes]
+    def pair_sum(k, j):
+        pair[k, j].wait_recv()
+        base = rows_of(j, c)
+        for h in range(2):
+            lanes = slice(LANES * h, LANES * h + LANES)
+            pa[k, j, h] = flat[k, pl.ds(base, HALF), lanes] + mine[k, j, 0:HALF, lanes]
+            pb[j, k, h] = flat[k, pl.ds(base + HALF, HALF), lanes] + mine[k, j, HALF:OWN, lanes]
 
     def relay(p, r, nxt, prv):
         return [send(p(0, 0), r.at[0], nxt), send(p(0, 1), r.at[1], prv)]
@@ -125,32 +124,34 @@
     a_relay, b_relay = [None] * 4, [None] * 4
 
     def launch(k):
-        pair_sum(k)
-        b_relay[k] = relay(b_slots[k], rb.at[k], z_next, z_prev)
-        if k == 0:
-            for j in range(4):
+        for j in range(4):
+            pair_sum(k, j)
+            if k == 0:
                 a_relay[j] = relay(a_slots[j], ra.at[j], y_next, y_prev)
-        b_sent[k] += [unmerged_next(b_slots[k], rb.at[k], z_next), unmerged_prev(b_slots[k], rb.at[k], z_prev)]
-        if k == 1:
-            for j in range(4):
+            if k == 1:
                 a_sent[j].append(unmerged_next(a_slots[j], ra.at[j], y_next))
-        if k == 2:
-            for j in range(4):
+            if k == 2:
                 a_sent[j].append(unmerged_prev(a_slots[j], ra.at[j], y_prev))
+            if j == 0:
+                b_relay[k] = relay(b_slots[k], rb.at[k], z_next, z_prev)
+            if j == 1:
+                b_sent[k].append(unmerged_next(b_slots[k], rb.at[k], z_next))
+            if j == 2:
+                b_sent[k].append(unmerged_prev(b_slots[k], rb.at[k], z_prev))
 
     turn(0)
     pl.semaphore_wait(barrier, 22)
     exchange(0)
     turn(1)
     exchange(1)
-    loads[4].wait()
-    pair_m = send(both_m.at[0], both_m.at[1], partner)
     launch(0)
     turn(2)
     exchange(2)
     launch(1)
     turn(3)
     exchange(3)
+    loads[4].wait()
+    pair_m = send(both_m.at[0], both_m.at[1], partner)
     launch(2)
     launch(3)
     for i in range(4):
@@ -259,7 +260,7 @@
                 lasts[n] += [send(q0.at[n, s], t0.at[n, s], ring[s]), send(q1.at[n, s], t1.at[n, s], ring[s])]
 
     ws = ((w00.at[c], w01.at[c]), (w10.at[c], w11.at[c]))
-    came, ring_parts, ring_relays, other = {}, {}, {}, []
+    came, spread, other = {}, {}, []
     for n, _, _, ring in colours:
         for copy in lasts[n]:
             copy.wait_recv()
@@ -269,21 +270,12 @@
             came[n, 4 - d] = [send(w.at[0, 0], w.at[0, 4 - d], ring[d]) for w in ws[n]]
 
     def around(n, s):
-        ring, (u0, u1) = colours[n][2], ws[n]
-        ring_parts[n, s] = [
-            send(u0.at[0, s], u0.at[3, s], ring[1]), send(u1.at[0, s], u1.at[1, s], ring[3]),
-            send(u1.at[0, s], u1.at[3, s], ring[1]), send(u0.at[0, s], u0.at[1, s], ring[3])]
-
-    def pass_on(n, s):
-        ring, (u0, u1) = colours[n][2], ws[n]
-        ring_parts[n, s][0].wait_recv()
-        first = send(u0.at[3, s], u0.at[2, s], ring[1])
-        ring_parts[n, s][1].wait_recv()
-        ring_relays[n, s] = [first, send(u1.at[1, s], u1.at[2, s], ring[3])]
-
-    def forward(n, slot):
+        for d in (2, 1, 3):
+            spread[n, 4 - d, s] = [send(w.at[0, s], w.at[4 - d, s], colours[n][2][d]) for w in ws[n]]
+
+    def forward(n, slot, s):
         for w in ws[n]:
-            other.append(send(w.at[slot], w.at[slot], partner))
+            other.append(send(w.at[slot, s], w.at[slot, s], partner))
 
     for n in range(2):
         around(n, 0)
@@ -292,25 +284,15 @@
             for copy in came[n, s]:
                 copy.wait_recv()
             around(n, s)
-        if s == 3:
+    for s in range(4):
+        for n in range(2):
+            forward(n, 0, s)
+    for s in (0, 1, 3, 2):
+        for slot in (1, 3, 2):
             for n in range(2):
-                pass_on(n, 0)
-    for n in range(2):
-        forward(n, 0)
-    for s in (1, 3, 2):
-        for n in range(2):
-            pass_on(n, s)
-    for n in range(2):
-        for s in range(4):
-            ring_parts[n, s][2].wait_recv()
-            ring_parts[n, s][3].wait_recv()
-        forward(n, 1)
-        forward(n, 3)
-    for n in range(2):
-        for s in range(4):
-            for copy in ring_relays[n, s]:
-                copy.wait_recv()
-        forward(n, 2)
+                for copy in spread[n, slot, s]:
+                    copy.wait_recv()
+                forward(n, slot, s)
     for copy in other:
         copy.wait_recv()
 

time: 121 us -> 118 us (0.975)
  Pallas kernels: 120 us -> 118 us
    pallas_call x1, Pallas kernels: 94.5 us -> 91.7 us  [gram_of(): pl.pallas_call(functools.partial(gram_kernel, count), out_shape=(jax.Shap...]
where the time goes in v4:
time: 118 us
  Pallas kernels  118 us (100%)
    pallas_call x1, Pallas kernels, gram_of(): pl.pallas_call(functools.partial(gram_kernel, count), out_shape=(jax.Shap...  91.7 us
    pallas_call x1, Pallas kernels, newton_schulz(): pl.pallas_call(newton_schulz_kernel, out_shape=[jax.ShapeDtypeStruct((OWN...  26 us

profile of v4, /device:TPU:1, one launch (start us, length us, event | category | flops | bytes accessed | tf_op | source)
XLA Modules:
  0.0 118.3 jit_solution(14164166396362530634)
XLA Ops:
  0.6 91.7 %gram_of_sum.1 = (f32[112,1024]{1,0:T(8,128)}, f32[112,1024]{1,0:T(8,128)}, f32[1024,1024]{1,0:T(8,128)}) custom-call(bf16[1024,3584]{1,0:T(8,128)(2,1)} %bitcast.10, f32[112,1024]{1,0:T(8,128)} %bitcast.11), custom_call_target="tpu_custom_call" | custom-call | tf_op jit(solution)/shard_map/gram_of_sum/pallas_call | solution.py:342
  92.4 26.0 %newton_schulz.1 = (f32[112,1024]{1,0:T(8,128)}, f32[112,1024]{1,0:T(8,128)}) custom-call(f32[1024,1024]{1,0:T(8,128)} %get-tuple-element.7.gram_ref, f32[112,1024]{1,0:T(8,128)} %get-tuple-element.8.start_ref, f32[112,1024]{1,0:T(8,128)} %get-tuple-element.9.new_ref), custom_call_target="tpu_custom_call" | custom-call | tf_op jit(solution)/shard_map/newton_schulz/pallas_call | solution.py:438

commit v5 on v4

--- a/solution.py
+++ b/solution.py
@@ -54,7 +54,7 @@
     spot = y * 4 + z
     plane = [(lax.rem(spot + d, 16) // 4, lax.rem(lax.rem(spot + d, 16), 4), c, x) for d in range(1, 16)]
     barrier = pltpu.get_barrier_semaphore()
-    for peer in x_line + plane:
+    for peer in x_line + [y_next, y_prev, z_next, z_prev]:
         pl.semaphore_signal(barrier, inc=1, device_id=peer, device_id_type=MESH)
 
     started = []
@@ -140,7 +140,7 @@
                 b_sent[k].append(unmerged_prev(b_slots[k], rb.at[k], z_prev))
 
     turn(0)
-    pl.semaphore_wait(barrier, 22)
+    pl.semaphore_wait(barrier, 11)
     exchange(0)
     turn(1)
     exchange(1)

time: 118 us -> 118 us (level)
  no operation moved by 1% of the time
where the time goes in v5:
time: 118 us
  Pallas kernels  117 us (99%)
    pallas_call x1, Pallas kernels, gram_of(): pl.pallas_call(functools.partial(gram_kernel, count), out_shape=(jax.Shap...  91.2 us
    pallas_call x1, Pallas kernels, newton_schulz(): pl.pallas_call(newton_schulz_kernel, out_shape=[jax.ShapeDtypeStruct((OWN...  26 us

profile of v5, /device:TPU:1, one launch (start us, length us, event | category | flops | bytes accessed | tf_op | source)
XLA Modules:
  0.0 117.8 jit_solution(11249031627639392067)
XLA Ops:
  0.6 91.2 %gram_of_sum.1 = (f32[112,1024]{1,0:T(8,128)}, f32[112,1024]{1,0:T(8,128)}, f32[1024,1024]{1,0:T(8,128)}) custom-call(bf16[1024,3584]{1,0:T(8,128)(2,1)} %bitcast.10, f32[112,1024]{1,0:T(8,128)} %bitcast.11), custom_call_target="tpu_custom_call" | custom-call | tf_op jit(solution)/shard_map/gram_of_sum/pallas_call | solution.py:342
  91.8 26.0 %newton_schulz.1 = (f32[112,1024]{1,0:T(8,128)}, f32[112,1024]{1,0:T(8,128)}) custom-call(f32[1024,1024]{1,0:T(8,128)} %get-tuple-element.7.gram_ref, f32[112,1024]{1,0:T(8,128)} %get-tuple-element.8.start_ref, f32[112,1024]{1,0:T(8,128)} %get-tuple-element.9.new_ref), custom_call_target="tpu_custom_call" | custom-call | tf_op jit(solution)/shard_map/newton_schulz/pallas_call | solution.py:438
